TPU v7x, 256 devices: a whole 4x4x8 slice. The times are simulated.
256 devices in a mesh: chan: 64 (over z, x_hi, y), sky: 4 (over x_lo, core).
Axes of the slice: x: 4 (x_hi: 2, x_lo: 2; x = x_hi * 2 + x_lo), y: 4, z: 8, core: 2. Of those that a mesh axis runs over, the one named last changes fastest.
Arguments:
- cube: float32 [512, 1024, 512], P('sky', 'chan'), may hold values from -6 to 6
- shifts: int32 [256], P('chan'), may hold values from -12 to 12
- halfwidth: int32 [256], P('chan'), may hold values from 1 to 4
- taps: float32 [1024, 9], P('chan'), may hold values from 0.1 to 1
- beam_rows: float32 [512, 512], replicated, as said below
- beam_cols: float32 [512, 512], replicated, as said below
Outputs:
- regridded: float32 [512, 1024, 512], P('sky', 'chan')
Inputs may be any that keep to these rules, and one draw needn't show every extreme that they name: beam_rows[i, j] is zero where |i - j| > 8; its diagonal exceeds the sum of the other entries of its row. beam_cols[i, j] is zero where |i - j| > 8; its diagonal exceeds the sum of the other entries of its row.
All inputs are finite; a program needn't handle non-finite values.
Results may differ from a plain program's by a relative error of at most 0.0003.
Values sent between devices are 32-bit elements; how exact they have to be, the bound alone decides.
A program may use at most 64 MiB of HBM per device.

v0:
```python
import jax
import jax.numpy as jnp
from jax import lax
from jax.sharding import PartitionSpec as P

BLK = 4
S_MAX = 12
RADIUS = 4


def with_halo(x, sides, width):
    for axis, dim in sides:
        size, length = (lax.axis_size(axis), x.shape[dim])
        up = [(i, (i + 1) % size) for i in range(size - 1)]
        down = [(j, i) for i, j in up]
        last = lax.slice_in_dim(x, length - width, length, axis=dim)
        first = lax.slice_in_dim(x, 0, width, axis=dim)
        before = lax.ppermute(last, axis, up)
        after = lax.ppermute(first, axis, down)
        x = jnp.concatenate([before, x, after], axis=dim)
    return x


def per_device(cube, shifts, halfwidth, taps, beam_rows, beam_cols):
    local_rows, chans, width = cube.shape
    reach = S_MAX + RADIUS
    taps_count = 2 * RADIUS + 1
    extended = with_halo(cube, (("chan", 1),), reach)
    chan_ids = jnp.arange(chans, dtype=jnp.int32)
    block_ids = chan_ids // BLK
    offsets = jnp.take(shifts, block_ids)
    limits = jnp.take(halfwidth, block_ids)
    tap_ids = jnp.arange(taps_count, dtype=jnp.int32)
    active = jnp.abs(tap_ids - RADIUS)[None, :] <= limits[:, None]
    masked = jnp.where(active, taps, jnp.float32(0.0))
    weights = masked / jnp.sum(masked, axis=1, keepdims=True)
    source = chan_ids[:, None] + reach + offsets[:, None] + tap_ids[None, :] - RADIUS
    positions = jnp.arange(chans + 2 * reach, dtype=jnp.int32)
    band = jnp.sum(
        jnp.where(
            source[:, :, None] == positions[None, None, :], weights[:, :, None], jnp.float32(0.0)
        ),
        axis=1,
    )
    interp = jnp.einsum("ce,hew->hcw", band, extended, precision=lax.Precision.HIGHEST)
    smoothed = jnp.einsum("hcw,vw->hcv", interp, beam_cols, precision=lax.Precision.HIGHEST)
    mixed = jnp.einsum(
        "gh,hcv->gcv",
        beam_rows,
        lax.all_to_all(smoothed, "sky", split_axis=1, concat_axis=0, tiled=True),
        precision=lax.Precision.HIGHEST,
    )
    return lax.all_to_all(mixed, "sky", split_axis=0, concat_axis=1, tiled=True)


def solution(mesh):
    placed = (P("sky", "chan", None), P("chan"), P("chan"), P("chan", None), P(), P())
    return jax.shard_map(
        per_device, mesh=mesh, in_specs=placed, out_specs=P("sky", "chan", None), check_vma=False
    )
```

profile of v0, /device:TPU:124, one launch (start us, length us, event | category | flops | bytes accessed | tf_op | source)
XLA Modules:
  0.0 261.4 jit_solution(18373305950960036583)
XLA Ops:
  0.0 0.0 copy-start
  0.0 4.8 %collective-permute-start = (f32[128,16,512]{2,1,0:T(8,128)}, f32[128,16,512]{2,1,0:T(8,128)}, u32[]{:S(2)}, u32[]{:S(2)}) collective-permute-start(f32[128,16,512]{2,1,0:T(8,128)} %param.8), channel_id=1, source_target_pairs={{0,4},{4,8},{8,12},{12,16},{16,20},{20,24},{24,28},{28,32},{32,36}... | collective-permute-start | bytes 12582920 | tf_op jit(solution)/shard_map/ppermute | solution.py:18
  4.8 1.9 collective-permute-start.1
  6.7 1.3 gather_fusion.1
  8.0 1.3 gather_fusion
  9.4 0.9 fusion.15
  10.3 0.8 fusion.14
  11.0 0.1 copy.15
  11.1 0.1 select_reduce_fusion
  11.3 83.6 %collective-permute-done = f32[128,16,512]{2,1,0:T(8,128)} collective-permute-done((f32[128,16,512]{2,1,0:T(8,128)}, f32[128,16,512]{2,1,0:T(8,128)}, u32[]{:S(2)}, u32[]{:S(2)}) %collective-permute-start) | collective-permute-done | bytes 4194336 | tf_op jit(solution)/shard_map/ppermute | solution.py:18
  94.9 9.8 %collective-permute-done.1 = f32[128,16,512]{2,1,0:T(8,128)} collective-permute-done((f32[128,16,512]{2,1,0:T(8,128)}, f32[128,16,512]{2,1,0:T(8,128)}, u32[]{:S(2)}, u32[]{:S(2)}) %collective-permute-start.1) | collective-permute-done | bytes 4194336 | tf_op jit(solution)/shard_map/ppermute | solution.py:19
  104.7 9.2 %fusion.8 = f32[128,16,512]{2,1,0:T(8,128)S(1)} fusion(f32[128,16,512]{2,1,0:T(8,128)} %collective-permute-done.1, f32[128,16,512]{2,1,0:T(8,128)} %param.8, f32[128,16,512]{2,1,0:T(8,128)} %collective-permute-done, f32[16,48]{1,0:T(8,128)S(1)} %select_reduce_fusion), kind=kOutput, calls=%fused_computation.10 | convolution fusion | flops 610271232 | bytes 16780288 | tf_op jit(solution)/shard_map/ce,hew->hcw/dot_general | solution.py:45
  114.0 0.0 copy-done
  114.0 9.3 %fusion.6 = f32[128,16,512]{2,0,1:T(8,128)S(1)} fusion(f32[128,16,512]{2,1,0:T(8,128)S(1)} %fusion.8, f32[512,512]{1,0:T(8,128)S(1)} %copy-done), kind=kOutput, calls=%fused_computation.8 | convolution fusion | flops 6442450944 | bytes 9437184 | tf_op jit(solution)/shard_map/hcw,vw->hcv/dot_general | solution.py:46
  123.3 51.6 %all_to_all.36 = f32[128,16,512]{2,0,1:T(8,128)} all-to-all(f32[128,16,512]{2,0,1:T(8,128)S(1)} %fusion.6), channel_id=1, replica_groups=mesh['chan'=64,'sky'=4] {'sky'}, dimensions={1} | all-to-all | bytes 8388608 | tf_op jit(solution)/shard_map/all_to_all | solution.py:50
  174.8 5.2 %copy.17 = f32[4,128,4,512]{1,0,3,2:T(4,128)} copy(f32[4,128,4,512]{3,1,2,0:T(8,128)} %bitcast.22) | data formatting | bytes 8388608 | tf_op jit(solution)/shard_map/all_to_all | solution.py:50
  180.1 0.0 copy-start.1
  180.1 5.6 %all_to_all.29 = f32[512,4,512]{0,2,1:T(8,128)} reshape(f32[4,128,4,512]{1,0,3,2:T(4,128)} %copy.17) | data formatting | bytes 8388608 | tf_op jit(solution)/shard_map/all_to_all | solution.py:50
  185.6 0.0 copy-done.1
  185.6 9.9 %convolution_bitcast_fusion = f32[512,4,512]{0,2,1:T(8,128)} fusion(f32[512,4,512]{0,2,1:T(8,128)} %all_to_all.29, f32[512,512]{1,0:T(8,128)S(1)} %copy-done.1), kind=kOutput, calls=%fused_computation.11 | convolution fusion | flops 6442450944 | bytes 9437184 | tf_op jit(solution)/shard_map/gh,hcv->gcv/dot_general | solution.py:47
  195.5 5.4 %copy.18 = f32[512,4,512]{2,1,0:T(4,128)} copy(f32[512,4,512]{0,2,1:T(8,128)} %convolution_bitcast_fusion) | data formatting | bytes 8388608 | tf_op jit(solution)/shard_map/gh,hcv->gcv/dot_general | solution.py:47
  200.9 51.9 %all_to_all.37 = f32[512,4,512]{2,1,0:T(4,128)S(1)} all-to-all(f32[512,4,512]{2,1,0:T(4,128)} %copy.18), channel_id=1, replica_groups=mesh['chan'=64,'sky'=4] {'sky'}, dimensions={0} | all-to-all | bytes 8388608 | tf_op jit(solution)/shard_map/all_to_all | solution.py:53
  252.8 3.3 %copy.19 = f32[128,4,4,512]{3,2,1,0:T(4,128)} copy(f32[128,4,4,512]{3,2,0,1:T(4,128)S(1)} %bitcast.23) | data formatting | bytes 8388608 | tf_op jit(solution)/shard_map/all_to_all | solution.py:53
  256.1 5.3 %all_to_all.33 = f32[128,16,512]{2,1,0:T(8,128)} reshape(f32[128,4,4,512]{3,2,1,0:T(4,128)} %copy.19) | data formatting | bytes 8388608 | tf_op jit(solution)/shard_map/all_to_all | solution.py:53
  (6 shorter events, 0.0 us)
Async XLA Ops:
  0.0 114.0 %copy-start = (f32[512,512]{1,0:T(8,128)S(1)}, f32[512,512]{1,0:T(8,128)}, u32[]{:S(2)}) copy-start(f32[512,512]{1,0:T(8,128)} %param.13) | copy-start | bytes 3145732
  0.0 94.9 %collective-permute-start = (f32[128,16,512]{2,1,0:T(8,128)}, f32[128,16,512]{2,1,0:T(8,128)}, u32[]{:S(2)}, u32[]{:S(2)}) collective-permute-start(f32[128,16,512]{2,1,0:T(8,128)} %param.8), channel_id=1, source_target_pairs={{0,4},{4,8},{8,12},{12,16},{16,20},{20,24},{24,28},{28,32},{32,36}... | collective-permute-start | bytes 12582920 | tf_op jit(solution)/shard_map/ppermute | solution.py:18
  4.8 100.0 %collective-permute-start.1 = (f32[128,16,512]{2,1,0:T(8,128)}, f32[128,16,512]{2,1,0:T(8,128)}, u32[]{:S(2)}, u32[]{:S(2)}) collective-permute-start(f32[128,16,512]{2,1,0:T(8,128)} %param.8), channel_id=1, source_target_pairs={{4,0},{8,4},{12,8},{16,12},{20,16},{24,20},{28,24},{32,28},{36,32}... | collective-permute-start | bytes 12582920 | tf_op jit(solution)/shard_map/ppermute | solution.py:19
  180.1 5.6 %copy-start.1 = (f32[512,512]{1,0:T(8,128)S(1)}, f32[512,512]{1,0:T(8,128)}, u32[]{:S(2)}) copy-start(f32[512,512]{1,0:T(8,128)} %param.12) | copy-start | bytes 3145732
where the time goes:
time: 262 us; the launch traced here: 261 us
  blocking collectives  103 us (39%)
  waiting for transfers between devices  93.5 us (36%)
  matrix products  28.4 us (11%)
  local copies, waits for them, and re-layouts  27.5 us (10%)
  starting transfers between devices  6.68 us (3%)
    ppermute x1, waiting for transfers between devices, with_halo(): before = lax.ppermute(last, axis, up)  83.6 us
    all_to_all x1, blocking collectives, per_device(): return lax.all_to_all(mixed, 'sky', split_axis=0, concat_axis=1, tiled=True)  51.9 us
    all_to_all x1, blocking collectives, per_device(): lax.all_to_all(smoothed, 'sky', split_axis=1, concat_axis=0, tiled=True)  51.6 us
    all_to_all x2, local copies, waits for them, and re-layouts, per_device(): lax.all_to_all(smoothed, 'sky', split_axis=1, concat_axis=0, tiled=True)  10.8 us
    dot_general x1, matrix products, per_device(): jnp.einsum('gh,hcv->gcv', beam_rows, lax.all_to_all(smoothed, 'sky', spli...  9.88 us
    ppermute x1, waiting for transfers between devices, with_halo(): after = lax.ppermute(first, axis, down)  9.84 us
    dot_general x1, matrix products, per_device(): jnp.einsum('hcw,vw->hcv', interp, beam_cols, precision=lax.Precision.HIGH...  9.29 us
    dot_general x1, matrix products, per_device(): jnp.einsum('ce,hew->hcw', band, extended, precision=lax.Precision.HIGHEST)  9.21 us
  transfers between devices with their start and end apart: 2, of which 2 were waited for; matrix products, arithmetic and copies ran while one was open for 2% of the time, Pallas kernels for 0%

commit v1 on v0

--- a/solution.py
+++ b/solution.py
@@ -50,7 +50,10 @@
         lax.all_to_all(smoothed, "sky", split_axis=1, concat_axis=0, tiled=True),
         precision=lax.Precision.HIGHEST,
     )
-    return lax.all_to_all(mixed, "sky", split_axis=0, concat_axis=1, tiled=True)
+    return jnp.concatenate(
+        lax.all_to_all(jnp.stack(jnp.split(mixed, lax.axis_size("sky"), axis=0)), "sky", 0, 0),
+        axis=1,
+    )
 
 
 def solution(mesh):

time: 262 us -> 253 us (0.966)
  local copies, waits for them, and re-layouts: 27.5 us -> 19.4 us
    all_to_all x2 -> x0, local copies, waits for them, and re-layouts: 8.52 us -> none  [per_device(): return lax.all_to_all(mixed, 'sky', split_axis=0, concat_axis=1, tiled=True)]
    reshape x0 -> x1, local copies, waits for them, and re-layouts: none -> 5.45 us  [per_device(): jnp.concatenate(lax.all_to_all(jnp.stack(jnp.split(mixed, lax.axis_size('...]
    dot_general x1 -> x0, local copies, waits for them, and re-layouts: 5.44 us -> none  [per_device(): jnp.einsum('gh,hcv->gcv', beam_rows, lax.all_to_all(smoothed, 'sky', spli...]
where the time goes in v1:
time: 253 us; the launch traced here: 252 us
  blocking collectives  103 us (41%)
  waiting for transfers between devices  93.5 us (37%)
  matrix products  27.1 us (11%)
  local copies, waits for them, and re-layouts  19.4 us (8%)
  starting transfers between devices  6.68 us (3%)
    ppermute x1, waiting for transfers between devices, with_halo(): before = lax.ppermute(last, axis, up)  83.6 us
    all_to_all x1, blocking collectives, per_device(): lax.all_to_all(smoothed, 'sky', split_axis=1, concat_axis=0, tiled=True)  51.6 us
    all_to_all x1, blocking collectives, per_device(): lax.all_to_all(jnp.stack(jnp.split(mixed, lax.axis_size('sky'), axis=0)),...  51.6 us
    all_to_all x2, local copies, waits for them, and re-layouts, per_device(): lax.all_to_all(smoothed, 'sky', split_axis=1, concat_axis=0, tiled=True)  10.8 us
    ppermute x1, waiting for transfers between devices, with_halo(): after = lax.ppermute(first, axis, down)  9.84 us
    dot_general x1, matrix products, per_device(): jnp.einsum('hcw,vw->hcv', interp, beam_cols, precision=lax.Precision.HIGH...  9.29 us
    dot_general x1, matrix products, per_device(): jnp.einsum('ce,hew->hcw', band, extended, precision=lax.Precision.HIGHEST)  9.21 us
    dot_general x1, matrix products, per_device(): jnp.einsum('gh,hcv->gcv', beam_rows, lax.all_to_all(smoothed, 'sky', spli...  8.56 us
  transfers between devices with their start and end apart: 2, of which 2 were waited for; matrix products, arithmetic and copies ran while one was open for 2% of the time, Pallas kernels for 0%

profile of v1, /device:TPU:124, one launch (start us, length us, event | category | flops | bytes accessed | tf_op | source)
XLA Modules:
  0.0 252.0 jit_solution(12776664280094749415)
XLA Ops:
  0.0 0.0 copy-start
  0.0 4.8 %collective-permute-start = (f32[128,16,512]{2,1,0:T(8,128)}, f32[128,16,512]{2,1,0:T(8,128)}, u32[]{:S(2)}, u32[]{:S(2)}) collective-permute-start(f32[128,16,512]{2,1,0:T(8,128)} %param.8), channel_id=1, source_target_pairs={{0,4},{4,8},{8,12},{12,16},{16,20},{20,24},{24,28},{28,32},{32,36}... | collective-permute-start | bytes 12582920 | tf_op jit(solution)/shard_map/ppermute | solution.py:18
  4.8 1.9 collective-permute-start.1
  6.7 1.3 gather_fusion.1
  8.0 1.3 gather_fusion
  9.4 0.9 fusion.15
  10.3 0.8 fusion.14
  11.0 0.1 copy.11
  11.1 0.1 select_reduce_fusion
  11.3 83.6 %collective-permute-done = f32[128,16,512]{2,1,0:T(8,128)} collective-permute-done((f32[128,16,512]{2,1,0:T(8,128)}, f32[128,16,512]{2,1,0:T(8,128)}, u32[]{:S(2)}, u32[]{:S(2)}) %collective-permute-start) | collective-permute-done | bytes 4194336 | tf_op jit(solution)/shard_map/ppermute | solution.py:18
  94.9 9.8 %collective-permute-done.1 = f32[128,16,512]{2,1,0:T(8,128)} collective-permute-done((f32[128,16,512]{2,1,0:T(8,128)}, f32[128,16,512]{2,1,0:T(8,128)}, u32[]{:S(2)}, u32[]{:S(2)}) %collective-permute-start.1) | collective-permute-done | bytes 4194336 | tf_op jit(solution)/shard_map/ppermute | solution.py:19
  104.7 9.2 %fusion.8 = f32[128,16,512]{2,1,0:T(8,128)S(1)} fusion(f32[128,16,512]{2,1,0:T(8,128)} %collective-permute-done.1, f32[128,16,512]{2,1,0:T(8,128)} %param.8, f32[128,16,512]{2,1,0:T(8,128)} %collective-permute-done, f32[16,48]{1,0:T(8,128)S(1)} %select_reduce_fusion), kind=kOutput, calls=%fused_computation.11 | convolution fusion | flops 610271232 | bytes 16780288 | tf_op jit(solution)/shard_map/ce,hew->hcw/dot_general | solution.py:45
  114.0 0.0 copy-done
  114.0 9.3 %fusion.6 = f32[128,16,512]{2,0,1:T(8,128)S(1)} fusion(f32[128,16,512]{2,1,0:T(8,128)S(1)} %fusion.8, f32[512,512]{1,0:T(8,128)S(1)} %copy-done), kind=kOutput, calls=%fused_computation.9 | convolution fusion | flops 6442450944 | bytes 9437184 | tf_op jit(solution)/shard_map/hcw,vw->hcv/dot_general | solution.py:46
  123.3 51.6 %all_to_all.23 = f32[128,16,512]{2,0,1:T(8,128)} all-to-all(f32[128,16,512]{2,0,1:T(8,128)S(1)} %fusion.6), channel_id=1, replica_groups=mesh['chan'=64,'sky'=4] {'sky'}, dimensions={1} | all-to-all | bytes 8388608 | tf_op jit(solution)/shard_map/all_to_all | solution.py:50
  174.8 5.2 %copy.13 = f32[4,128,4,512]{1,0,3,2:T(4,128)} copy(f32[4,128,4,512]{3,1,2,0:T(8,128)} %bitcast.30) | data formatting | bytes 8388608 | tf_op jit(solution)/shard_map/all_to_all | solution.py:50
  180.1 0.0 copy-start.1
  180.1 5.6 %all_to_all.19 = f32[512,4,512]{0,2,1:T(8,128)} reshape(f32[4,128,4,512]{1,0,3,2:T(4,128)} %copy.13) | data formatting | bytes 8388608 | tf_op jit(solution)/shard_map/all_to_all | solution.py:50
  185.6 0.0 copy-done.1
  185.6 8.6 %convolution_bitcast_fusion = f32[512,4,512]{0,2,1:T(8,128)S(1)} fusion(f32[512,4,512]{0,2,1:T(8,128)} %all_to_all.19, f32[512,512]{1,0:T(8,128)S(1)} %copy-done.1), kind=kOutput, calls=%fused_computation.12 | convolution fusion | flops 6442450944 | bytes 9437184 | tf_op jit(solution)/shard_map/gh,hcv->gcv/dot_general | solution.py:47
  194.2 0.4 slice_bitcast_fusion.3
  194.6 0.4 pad_maximum_fusion
  195.0 51.6 %all_to_all.24 = f32[4,128,4,512]{1,3,2,0:T(8,128)} all-to-all(f32[4,128,4,512]{1,3,2,0:T(8,128)S(1)} %pad_maximum_fusion), channel_id=1, replica_groups=mesh['chan'=64,'sky'=4] {'sky'}, dimensions={0} | all-to-all | bytes 8388608 | tf_op jit(solution)/shard_map/all_to_all | solution.py:54
  246.6 5.4 %copy.14 = f32[128,16,512]{2,1,0:T(8,128)} copy(f32[128,16,512]{0,2,1:T(8,128)} %bitcast.31) | data formatting | bytes 8388608 | tf_op jit(solution)/shard_map/reshape | solution.py:53
  (6 shorter events, 0.0 us)
Async XLA Ops:
  0.0 114.0 %copy-start = (f32[512,512]{1,0:T(8,128)S(1)}, f32[512,512]{1,0:T(8,128)}, u32[]{:S(2)}) copy-start(f32[512,512]{1,0:T(8,128)} %param.13) | copy-start | bytes 3145732
  0.0 94.9 %collective-permute-start = (f32[128,16,512]{2,1,0:T(8,128)}, f32[128,16,512]{2,1,0:T(8,128)}, u32[]{:S(2)}, u32[]{:S(2)}) collective-permute-start(f32[128,16,512]{2,1,0:T(8,128)} %param.8), channel_id=1, source_target_pairs={{0,4},{4,8},{8,12},{12,16},{16,20},{20,24},{24,28},{28,32},{32,36}... | collective-permute-start | bytes 12582920 | tf_op jit(solution)/shard_map/ppermute | solution.py:18
  4.8 100.0 %collective-permute-start.1 = (f32[128,16,512]{2,1,0:T(8,128)}, f32[128,16,512]{2,1,0:T(8,128)}, u32[]{:S(2)}, u32[]{:S(2)}) collective-permute-start(f32[128,16,512]{2,1,0:T(8,128)} %param.8), channel_id=1, source_target_pairs={{4,0},{8,4},{12,8},{16,12},{20,16},{24,20},{28,24},{32,28},{36,32}... | collective-permute-start | bytes 12582920 | tf_op jit(solution)/shard_map/ppermute | solution.py:19
  180.1 5.6 %copy-start.1 = (f32[512,512]{1,0:T(8,128)S(1)}, f32[512,512]{1,0:T(8,128)}, u32[]{:S(2)}) copy-start(f32[512,512]{1,0:T(8,128)} %param.12) | copy-start | bytes 3145732
